TPU v7x, 32 devices: a whole 2x2x4 slice. The times are simulated.
32 devices in a mesh: gy: 4 (over x, core), gx: 4 (over z), probe: 2 (over y).
Axes of the slice: x: 2, y: 2, z: 4, core: 2. Of those that a mesh axis runs over, the one named last changes fastest.
Arguments:
- state: bfloat16 [4, 16, 16, 640], P(None, 'gy', 'gx'), may hold values from -6 to 6
- probe_signs: int32 [4, 4, 16, 16, 640], P('probe', None, 'gy', 'gx'), may hold values from -1 to 1, as said below
- timesteps: int32 [4], replicated, may hold values from 0 to 999
- time_table: float32 [1000, 640], replicated, may hold values from -4 to 4
- gn_gain: float32 [640], replicated, may hold values from 0.5 to 1.5
- gn_shift: float32 [640], replicated, may hold values from -3 to 3
- conv_weight: bfloat16 [9, 640, 640], P(None, 'probe'), may hold values from -0.078125 to 0.078125
- conv_bias: float32 [640], replicated, may hold values from -3 to 3
Outputs:
- next_state: bfloat16 [4, 16, 16, 640], P(None, 'gy', 'gx')
- logp_delta: float32 [4], replicated
Inputs may be any that keep to these rules, and one draw needn't show every extreme that they name: `probe_signs`: every entry is -1 or 1.
All inputs are finite; a program needn't handle non-finite values.
Results may differ from a plain program's by a relative error of at most 0.0034.
Values may be sent and summed in bfloat16 or wider, within the bound.
A program may use at most 64 MiB of HBM per device.

v0:
```python
import jax
import jax.numpy as jnp
from jax import lax
from jax.sharding import PartitionSpec as P

GROUPS = 32


def with_halo(block, sides, width):
    for axis, dim in sides:
        count = lax.axis_size(axis)
        forward = [(i, i + 1) for i in range(count - 1)]
        backward = [(target, source) for source, target in forward]
        low = lax.ppermute(
            lax.slice_in_dim(block, block.shape[dim] - width, None, axis=dim), axis, forward
        )
        high = lax.ppermute(lax.slice_in_dim(block, 0, width, axis=dim), axis, backward)
        block = jnp.concatenate([low, block, high], axis=dim)
    return block


def local_conv(padded, weight, height, width):
    count = padded.shape[0]
    chans = padded.shape[3]
    total = jnp.zeros((count * height * width, weight.shape[2]), jnp.float32)
    for tap in range(9):
        row_off = tap // 3
        col_off = tap % 3
        window = padded[:, row_off : row_off + height, col_off : col_off + width, :].reshape(
            -1, chans
        )
        total = total + jnp.dot(window, weight[tap], preferred_element_type=jnp.float32)
    return total


def travelling_probes(
    state, probe_signs, timesteps, time_table, gn_gain, gn_shift, conv_weight, conv_bias
):
    batch, tile_h, tile_w, chans = state.shape
    share = conv_weight.shape[1]
    group_width = chans // GROUPS
    ny, nx = (lax.axis_size("gy"), lax.axis_size("gx"))
    count = tile_h * ny * tile_w * nx * group_width
    xf = state.astype(jnp.float32)
    signs = lax.all_gather(probe_signs.astype(jnp.bfloat16), "probe", axis=0, tiled=True)
    probes = signs.shape[0]
    first = lax.axis_index("probe") * share

    def mine(array):
        return lax.dynamic_slice_in_dim(array, first, share, axis=array.ndim - 1)

    stacked = jnp.concatenate([state[None], signs], axis=0)
    stacked = mine(stacked).reshape((1 + probes) * batch, tile_h, tile_w, share)
    padded = with_halo(stacked, (("gy", 1), ("gx", 2)), 1)
    padded = padded.reshape(1 + probes, batch, tile_h + 2, tile_w + 2, share).astype(jnp.float32)
    cells_x = jnp.stack([jnp.sum(xf, axis=(1, 2)), jnp.sum(xf * xf, axis=(1, 2))])
    signs_f = signs.astype(jnp.float32)
    cells_u = jnp.stack([jnp.sum(signs_f, axis=(2, 3)), jnp.sum(signs_f * xf[None], axis=(2, 3))])
    cells = jnp.concatenate([cells_x, cells_u.reshape(2 * probes, batch, chans)], axis=0)
    sums = jnp.sum(cells.reshape(2 + 2 * probes, batch, GROUPS, group_width), axis=3)
    sums = lax.psum(sums, ("gy", "gx")) / count
    mean_x, mean_xx = (sums[0], sums[1])
    mean_u, cross = (sums[2 : 2 + probes], sums[2 + probes :])
    sigma = jnp.sqrt(mean_xx - mean_x * mean_x + 1e-05)
    mean_cu = cross - mean_x[None] * mean_u
    inv = 1.0 / sigma
    table = jnp.concatenate([mean_x[None], inv[None], mean_u, mean_cu * (inv * inv * inv)], axis=0)
    table = mine(jnp.repeat(table, group_width, axis=2))[:, :, None, None, :]
    onehot = (
        timesteps[:, None] == jnp.arange(time_table.shape[0], dtype=jnp.int32)[None, :]
    ).astype(jnp.float32)
    embed = jnp.dot(onehot, time_table, precision=lax.Precision.HIGHEST)
    offset = mine(gn_shift + embed)[:, None, None, :]
    gain = mine(gn_gain)
    centered = padded[0] - table[0]
    pre = centered * table[1] * gain + offset
    sig = jax.nn.sigmoid(pre)
    rows = lax.axis_index("gy") * tile_h - 1 + jnp.arange(tile_h + 2)
    cols = lax.axis_index("gx") * tile_w - 1 + jnp.arange(tile_w + 2)
    inside = ((rows >= 0) & (rows < tile_h * ny))[:, None] & ((cols >= 0) & (cols < tile_w * nx))[
        None, :
    ]
    inside = inside[:, :, None]
    hidden = jnp.where(inside, pre * sig, 0.0).astype(jnp.bfloat16)
    slope = jnp.where(inside, sig * (1.0 + pre * (1.0 - sig)) * gain, 0.0)
    dnormal = (padded[1:] - table[2 : 2 + probes]) * table[1] - centered * table[2 + probes :]
    dhidden = (slope[None] * dnormal).astype(jnp.bfloat16)
    velocity = local_conv(hidden, conv_weight, tile_h, tile_w)
    velocity = lax.psum(velocity, "probe").reshape(batch, tile_h, tile_w, chans) + conv_bias
    next_state = (xf + 0.25 * velocity).astype(jnp.bfloat16)
    tangent = local_conv(
        dhidden.reshape(probes * batch, tile_h + 2, tile_w + 2, share), conv_weight, tile_h, tile_w
    ).reshape(signs.shape)
    total = lax.psum(jnp.sum(signs_f * tangent, axis=(0, 2, 3, 4)), ("gy", "gx", "probe"))
    return (next_state, -0.25 / probes * total)


def gathered_weights(
    state, probe_signs, timesteps, time_table, gn_gain, gn_shift, conv_weight, conv_bias
):
    batch, tile_h, tile_w, chans = state.shape
    probes_here = probe_signs.shape[0]
    group_width = chans // GROUPS
    count = tile_h * lax.axis_size("gy") * tile_w * lax.axis_size("gx") * group_width
    xf = state.astype(jnp.float32)
    signs = probe_signs.astype(jnp.float32)
    grouped = xf.reshape(batch, tile_h, tile_w, GROUPS, group_width)
    signs_grouped = signs.reshape(probes_here, batch, tile_h, tile_w, GROUPS, group_width)
    sum_x = jnp.sum(grouped, axis=(1, 2, 4))
    sum_xx = jnp.sum(grouped * grouped, axis=(1, 2, 4))
    sum_u = jnp.sum(signs_grouped, axis=(2, 3, 5))
    cross = jnp.sum(signs_grouped * grouped[None], axis=(2, 3, 5))
    sum_x, sum_xx, sum_u, cross = lax.psum((sum_x, sum_xx, sum_u, cross), ("gy", "gx"))
    mean_x = sum_x / count
    centered = grouped - mean_x[:, None, None, :, None]
    sum_cu = cross - mean_x[None] * sum_u
    var_x = sum_xx / count - mean_x * mean_x
    sigma = jnp.sqrt(var_x + 1e-05)[:, None, None, :, None]
    normal = (centered / sigma).reshape(batch, tile_h, tile_w, chans)
    mean_u = (sum_u / count)[:, :, None, None, :, None]
    mean_cu = (sum_cu / count)[:, :, None, None, :, None]
    dnormal = (signs_grouped - mean_u) / sigma[None] - centered[None] * mean_cu / (
        sigma * sigma * sigma
    )[None]
    dnormal = dnormal.reshape(probes_here, batch, tile_h, tile_w, chans)
    onehot = (
        timesteps[:, None] == jnp.arange(time_table.shape[0], dtype=jnp.int32)[None, :]
    ).astype(jnp.float32)
    embed = jnp.dot(onehot, time_table, precision=lax.Precision.HIGHEST)
    pre = normal * gn_gain + gn_shift + embed[:, None, None, :]
    sig = jax.nn.sigmoid(pre)
    hidden = (pre * sig).astype(jnp.bfloat16)
    slope = sig * (1.0 + pre * (1.0 - sig)) * gn_gain
    dhidden = (slope[None] * dnormal).astype(jnp.bfloat16)
    flat_tangents = dhidden.reshape(probes_here * batch, tile_h, tile_w, chans)
    stacked = jnp.concatenate([hidden, flat_tangents], axis=0)
    items = stacked.shape[0]
    padded = with_halo(stacked, (("gy", 1), ("gx", 2)), 1)
    summed = local_conv(
        padded, lax.all_gather(conv_weight, "probe", axis=1, tiled=True), tile_h, tile_w
    )
    conv_out = summed.reshape(items, tile_h, tile_w, chans)
    conv_primal = conv_out[:batch]
    tangent = conv_out[batch:].reshape(probes_here, batch, tile_h, tile_w, chans)
    partial_sum = jnp.sum(signs * tangent, axis=(0, 2, 3, 4))
    velocity = conv_primal + conv_bias
    next_state = (xf + 0.25 * velocity).astype(jnp.bfloat16)
    total = lax.psum(partial_sum, ("gy", "gx", "probe"))
    logp_delta = -0.25 / (probes_here * lax.axis_size("probe")) * total
    return (next_state, logp_delta)


def solution(mesh):

    def body(*args):
        wide = args[6].shape[1] >= 128
        return (travelling_probes if wide else gathered_weights)(*args)

    in_specs = (
        P(None, "gy", "gx", None),
        P("probe", None, "gy", "gx", None),
        P(),
        P(),
        P(),
        P(),
        P(None, "probe", None),
        P(),
    )
    out_specs = (P(None, "gy", "gx", None), P())
    return jax.shard_map(body, mesh=mesh, in_specs=in_specs, out_specs=out_specs, check_vma=False)
```

profile of v0, /device:TPU:0, one launch (start us, length us, event | category | flops | bytes accessed | tf_op | source)
XLA Modules:
  0.0 215.1 jit_solution(14110770725235641444)
XLA Ops:
  8.4 7.9 %all_gather.3 = bf16[4,4,4,4,640]{4,3,2,1,0:T(4,128)(2,1)S(1)} all-gather(bf16[2,4,4,4,640]{4,3,2,1,0:T(4,128)(2,1)S(1)} %convert_element_type.24), channel_id=1, replica_groups=mesh['gy'=4,'gx'=4,'probe'=2] {'probe'}, dimensions={0}, use_global_device_ids=true | all-gather | bytes 491520 | tf_op jit(solution)/shard_map/all_gather | solution.py:45
  19.4 3.0 %collective-permute-start = (bf16[20,1,4,320]{3,2,1,0:T(4,128)(2,1)}, bf16[20,1,4,320]{3,2,1,0:T(4,128)(2,1)S(1)}, u32[]{:S(2)}, u32[]{:S(2)}) collective-permute-start(bf16[20,1,4,320]{3,2,1,0:T(4,128)(2,1)} %get-tuple-element.21), channel_id=1, source_target_pairs={{0,8},{8,16},{16,24},{1,9},{9,17},{17,25},{2,10},{10,18},{18,26},{... | collective-permute-start | bytes 153608 | tf_op jit(solution)/shard_map/ppermute | solution.py:14
  28.4 61.5 %psum.21 = f32[10,4,32]{2,1,0:T(4,128)S(1)} all-reduce(f32[10,4,32]{2,1,0:T(4,128)S(1)} %maximum_reduce_fusion), channel_id=1, replica_groups=mesh['gy'=4,'gx'=4,'probe'=2] {'gy','gx'}, use_global_device_ids=true, to_apply=%region_5.0 | all-reduce | flops 1280 | bytes 10240 | tf_op jit(solution)/shard_map/psum | solution.py:61
  91.1 1.5 reshape.118
  97.6 4.6 %collective-permute-start.2 = (bf16[20,6,1,320]{3,2,1,0:T(2,128)(2,1)S(1)}, bf16[20,6,1,320]{3,2,1,0:T(2,128)(2,1)S(1)}, u32[]{:S(2)}, u32[]{:S(2)}) collective-permute-start(bf16[20,6,1,320]{3,2,1,0:T(2,128)(2,1)S(1)} %get-tuple-element.19), channel_id=1, source_target_pairs={{0,2},{2,4},{4,6},{1,3},{3,5},{5,7},{8,10},{10,12},{12,14},{9,11},... | collective-permute-start | bytes 230408 | tf_op jit(solution)/shard_map/ppermute | solution.py:14
  102.3 1.5 collective-permute-done.3
  103.7 1.5 collective-permute-done.2
  105.2 1.7 select_bitcast_fusion
  131.6 1.9 convolution_add_fusion.8
  133.5 1.6 reshape.128
  135.1 1.5 fusion.2
  137.8 1.7 fusion.64
  141.8 1.7 reshape.131
  143.4 1.7 reshape.132
  145.1 1.7 reshape.133
  146.8 1.7 reshape.134
  148.5 1.7 reshape.135
  150.2 1.7 reshape.136
  151.9 1.7 reshape.137
  153.6 1.7 reshape.138
  155.3 1.6 convolution_add_fusion.7
  156.9 1.5 convolution_add_fusion.6
  164.0 42.0 %psum.23 = f32[4]{0:T(128)S(1)} all-reduce(f32[4]{0:T(128)S(1)} %fusion.1), channel_id=1, replica_groups=mesh['gy'=4,'gx'=4,'probe'=2] {'gy','gx','probe'}, use_global_device_ids=true, to_apply=%region_8.9 | all-reduce | flops 4 | bytes 32 | tf_op jit(solution)/shard_map/psum | solution.py:94
  206.6 1.7 add_convert_fusion
  (99 shorter events, 50.5 us)
Async XLA Ops:
  7.2 85.5 %copy-start = (f32[1000,640]{1,0:T(8,128)S(1)}, f32[1000,640]{1,0:T(8,128)}, u32[]{:S(2)}) copy-start(f32[1000,640]{1,0:T(8,128)} %param.11) | copy-start | bytes 7680004
  7.2 85.5 %copy-start.16 = (s32[4]{0:T(128)S(1)}, s32[4]{0:T(128)}, u32[]{:S(2)}) copy-start(s32[4]{0:T(128)} %param.10) | copy-start | bytes 52
  7.2 199.4 %all-reduce.2.cloned.1.call-start = ((), (), s32[]{:S(2)}) async-start(), calls=%async_computation | async-start | bytes 327680 | tf_op jit(solution)/shard_map/psum | solution.py:89
  17.4 78.3 %copy-start.15 = (f32[640]{0:T(1024)S(1)}, f32[640]{0:T(1024)}, u32[]{:S(2)}) copy-start(f32[640]{0:T(1024)} %param.12) | copy-start | bytes 7684
  18.1 77.7 %collective-permute-start.1 = (bf16[20,1,4,320]{3,2,1,0:T(4,128)(2,1)}, bf16[20,1,4,320]{3,2,1,0:T(4,128)(2,1)S(1)}, u32[]{:S(2)}, u32[]{:S(2)}) collective-permute-start(bf16[20,1,4,320]{3,2,1,0:T(4,128)(2,1)} %get-tuple-element.22), channel_id=1, source_target_pairs={{8,0},{16,8},{24,16},{9,1},{17,9},{25,17},{10,2},{18,10},{26,18},{... | collective-permute-start | bytes 153608 | tf_op jit(solution)/shard_map/ppermute | solution.py:17
  19.4 76.4 %collective-permute-start = (bf16[20,1,4,320]{3,2,1,0:T(4,128)(2,1)}, bf16[20,1,4,320]{3,2,1,0:T(4,128)(2,1)S(1)}, u32[]{:S(2)}, u32[]{:S(2)}) collective-permute-start(bf16[20,1,4,320]{3,2,1,0:T(4,128)(2,1)} %get-tuple-element.21), channel_id=1, source_target_pairs={{0,8},{8,16},{16,24},{1,9},{9,17},{17,25},{2,10},{10,18},{18,26},{... | collective-permute-start | bytes 153608 | tf_op jit(solution)/shard_map/ppermute | solution.py:14
  96.3 7.4 %collective-permute-start.3 = (bf16[20,6,1,320]{3,2,1,0:T(2,128)(2,1)S(1)}, bf16[20,6,1,320]{3,2,1,0:T(2,128)(2,1)S(1)}, u32[]{:S(2)}, u32[]{:S(2)}) collective-permute-start(bf16[20,6,1,320]{3,2,1,0:T(2,128)(2,1)S(1)} %get-tuple-element.20), channel_id=1, source_target_pairs={{2,0},{4,2},{6,4},{3,1},{5,3},{7,5},{10,8},{12,10},{14,12},{11,9},... | collective-permute-start | bytes 230408 | tf_op jit(solution)/shard_map/ppermute | solution.py:17
  97.6 7.6 %collective-permute-start.2 = (bf16[20,6,1,320]{3,2,1,0:T(2,128)(2,1)S(1)}, bf16[20,6,1,320]{3,2,1,0:T(2,128)(2,1)S(1)}, u32[]{:S(2)}, u32[]{:S(2)}) collective-permute-start(bf16[20,6,1,320]{3,2,1,0:T(2,128)(2,1)S(1)} %get-tuple-element.19), channel_id=1, source_target_pairs={{0,2},{2,4},{4,6},{1,3},{3,5},{5,7},{8,10},{10,12},{12,14},{9,11},... | collective-permute-start | bytes 230408 | tf_op jit(solution)/shard_map/ppermute | solution.py:14
  102.2 4.7 %copy-start.13 = (f32[4,320]{1,0:T(4,128)}, f32[4,320]{1,0:T(4,128)S(1)}, u32[]{:S(2)}) copy-start(f32[4,320]{1,0:T(4,128)S(1)} %get-tuple-element.35) | copy-start | bytes 15364
  103.7 3.2 %copy-start.7 = (bf16[20,6,1,320]{3,2,1,0:T(2,128)(2,1)}, bf16[20,6,1,320]{3,2,1,0:T(2,128)(2,1)S(1)}, u32[]{:S(2)}) copy-start(bf16[20,6,1,320]{3,2,1,0:T(2,128)(2,1)S(1)} %collective-permute-done.3) | copy-start | bytes 230404
  105.2 2.5 %copy-start.8 = (bf16[20,6,1,320]{3,2,1,0:T(2,128)(2,1)}, bf16[20,6,1,320]{3,2,1,0:T(2,128)(2,1)S(1)}, u32[]{:S(2)}) copy-start(bf16[20,6,1,320]{3,2,1,0:T(2,128)(2,1)S(1)} %collective-permute-done.2) | copy-start | bytes 230404
  121.6 6.3 %copy-start.12 = (bf16[64,320]{1,0:T(8,128)(2,1)S(1)}, bf16[64,320]{1,0:T(8,128)(2,1)}, u32[]{:S(2)}) copy-start(bf16[64,320]{1,0:T(8,128)(2,1)} %reshape.124) | copy-start | bytes 122884
  121.6 7.5 %copy-start.11 = (bf16[64,320]{1,0:T(8,128)(2,1)S(1)}, bf16[64,320]{1,0:T(8,128)(2,1)}, u32[]{:S(2)}) copy-start(bf16[64,320]{1,0:T(8,128)(2,1)} %reshape.125) | copy-start | bytes 122884
  121.6 8.7 %copy-start.9 = (bf16[64,320]{1,0:T(8,128)(2,1)S(1)}, bf16[64,320]{1,0:T(8,128)(2,1)}, u32[]{:S(2)}) copy-start(bf16[64,320]{1,0:T(8,128)(2,1)} %reshape.126) | copy-start | bytes 122884
  121.6 9.9 %copy-start.10 = (bf16[64,320]{1,0:T(8,128)(2,1)S(1)}, bf16[64,320]{1,0:T(8,128)(2,1)}, u32[]{:S(2)}) copy-start(bf16[64,320]{1,0:T(8,128)(2,1)} %reshape.127) | copy-start | bytes 122884
  155.3 3.1 %copy-start.1 = (bf16[9,320,640]{2,1,0:T(8,128)(2,1)S(1)}, bf16[9,320,640]{2,1,0:T(8,128)(2,1)}, u32[]{:S(2)}) copy-start(bf16[9,320,640]{2,1,0:T(8,128)(2,1)} %param.14) | copy-start | bytes 11059204
  155.3 4.5 %copy-start.6 = (bf16[256,320]{1,0:T(8,128)(2,1)S(1)}, bf16[256,320]{1,0:T(8,128)(2,1)}, u32[]{:S(2)}) copy-start(bf16[256,320]{1,0:T(8,128)(2,1)} %reshape.134) | copy-start | bytes 491524
  155.3 4.8 %copy-start.5 = (bf16[256,320]{1,0:T(8,128)(2,1)S(1)}, bf16[256,320]{1,0:T(8,128)(2,1)}, u32[]{:S(2)}) copy-start(bf16[256,320]{1,0:T(8,128)(2,1)} %reshape.135) | copy-start | bytes 491524
  156.9 3.6 %copy-start.4 = (bf16[256,320]{1,0:T(8,128)(2,1)S(1)}, bf16[256,320]{1,0:T(8,128)(2,1)}, u32[]{:S(2)}) copy-start(bf16[256,320]{1,0:T(8,128)(2,1)} %reshape.136) | copy-start | bytes 491524
  158.4 2.5 %copy-start.2 = (bf16[256,320]{1,0:T(8,128)(2,1)S(1)}, bf16[256,320]{1,0:T(8,128)(2,1)}, u32[]{:S(2)}) copy-start(bf16[256,320]{1,0:T(8,128)(2,1)} %reshape.137) | copy-start | bytes 491524
  159.7 1.5 copy-start.3
  160.5 46.1 %copy-start.14 = (f32[640]{0:T(1024)S(1)}, f32[640]{0:T(1024)}, u32[]{:S(2)}) copy-start(f32[640]{0:T(1024)} %param.15) | copy-start | bytes 7684
Sparse Core Ops, SparseCore 0:
  164.2 23.1 all-reduce.1
where the time goes:
time: 217 us; the launch traced here: 215 us
  blocking collectives  111 us (51%)
  local copies, waits for them, and re-layouts  39.6 us (18%)
  matrix products  21.1 us (10%)
  other arithmetic  15.3 us (7%)
  between operations  14.5 us (7%)
  starting transfers between devices  10.2 us (5%)
  waiting for transfers between devices  2.96 us (1%)
    psum x1, blocking collectives, travelling_probes(): sums = lax.psum(sums, ('gy', 'gx')) / count  61.5 us
    psum x1, blocking collectives, travelling_probes(): lax.psum(jnp.sum(signs_f * tangent, axis=(0, 2, 3, 4)), ('gy', 'gx', 'pro...  42 us
    reshape x18, local copies, waits for them, and re-layouts, local_conv(): padded[:, row_off:row_off + height, col_off:col_off + width, :]  27.3 us
    dot_general x18, matrix products, local_conv(): jnp.dot(window, weight[tap], preferred_element_type=jnp.float32)  20.2 us
    all_gather x1, blocking collectives, travelling_probes(): lax.all_gather(probe_signs.astype(jnp.bfloat16), 'probe', axis=0, tiled=T...  7.85 us
    ppermute x2, starting transfers between devices, with_halo(): lax.ppermute(lax.slice_in_dim(block, block.shape[dim] - width, None, axis...  7.59 us
  transfers between devices with their start and end apart: 5, of which 2 were waited for; matrix products, arithmetic and copies ran while one was open for 6% of the time, Pallas kernels for 0%

commit v1 on v0

--- a/solution.py
+++ b/solution.py
@@ -4,6 +4,11 @@
 from jax.sharding import PartitionSpec as P
 
 GROUPS = 32
+
+
+def finish_marks_on_mesh(local_x):
+    moved = jnp.sum(lax.all_gather(local_x, axis_name=("gy", "gx")), axis=0)
+    return moved
 
 
 def with_halo(block, sides, width):
@@ -58,7 +63,7 @@
     cells_u = jnp.stack([jnp.sum(signs_f, axis=(2, 3)), jnp.sum(signs_f * xf[None], axis=(2, 3))])
     cells = jnp.concatenate([cells_x, cells_u.reshape(2 * probes, batch, chans)], axis=0)
     sums = jnp.sum(cells.reshape(2 + 2 * probes, batch, GROUPS, group_width), axis=3)
-    sums = lax.psum(sums, ("gy", "gx")) / count
+    sums = finish_marks_on_mesh(sums) / count
     mean_x, mean_xx = (sums[0], sums[1])
     mean_u, cross = (sums[2 : 2 + probes], sums[2 + probes :])
     sigma = jnp.sqrt(mean_xx - mean_x * mean_x + 1e-05)

time: 217 us -> 191 us (0.88)
  blocking collectives: 111 us -> 84.6 us
    psum x1 -> x0, blocking collectives: 61.5 us -> none  [travelling_probes(): sums = lax.psum(sums, ('gy', 'gx')) / count]
    all_gather x0 -> x1, blocking collectives: none -> 34.6 us  [finish_marks_on_mesh(): moved = jnp.sum(lax.all_gather(local_x, axis_name=('gy', 'gx')), axis=0)]
where the time goes in v1:
time: 191 us; the launch traced here: 189 us
  blocking collectives  84.6 us (44%)
  local copies, waits for them, and re-layouts  39.6 us (21%)
  matrix products  21.2 us (11%)
  other arithmetic  15.6 us (8%)
  between operations  14.4 us (8%)
  starting transfers between devices  10.8 us (6%)
  waiting for transfers between devices  2.96 us (2%)
    psum x1, blocking collectives, travelling_probes(): lax.psum(jnp.sum(signs_f * tangent, axis=(0, 2, 3, 4)), ('gy', 'gx', 'pro...  42.1 us
    all_gather x1, blocking collectives, finish_marks_on_mesh(): moved = jnp.sum(lax.all_gather(local_x, axis_name=('gy', 'gx')), axis=0)  34.6 us
    reshape x18, local copies, waits for them, and re-layouts, local_conv(): padded[:, row_off:row_off + height, col_off:col_off + width, :]  27.3 us
    dot_general x18, matrix products, local_conv(): jnp.dot(window, weight[tap], preferred_element_type=jnp.float32)  20.2 us
    ppermute x2, starting transfers between devices, with_halo(): lax.ppermute(lax.slice_in_dim(block, block.shape[dim] - width, None, axis...  8.22 us
    all_gather x1, blocking collectives, travelling_probes(): lax.all_gather(probe_signs.astype(jnp.bfloat16), 'probe', axis=0, tiled=T...  7.85 us
  transfers between devices with their start and end apart: 5, of which 2 were waited for; matrix products, arithmetic and copies ran while one was open for 6% of the time, Pallas kernels for 0%

profile of v1, /device:TPU:0, one launch (start us, length us, event | category | flops | bytes accessed | tf_op | source)
XLA Modules:
  0.0 189.2 jit_solution(17003219712620143055)
XLA Ops:
  8.4 7.9 %all_gather.9 = bf16[4,4,4,4,640]{4,3,2,1,0:T(4,128)(2,1)S(1)} all-gather(bf16[2,4,4,4,640]{4,3,2,1,0:T(4,128)(2,1)S(1)} %convert_element_type.24), channel_id=1, replica_groups=mesh['gy'=4,'gx'=4,'probe'=2] {'probe'}, dimensions={0}, use_global_device_ids=true | all-gather | bytes 491520 | tf_op jit(solution)/shard_map/all_gather | solution.py:50
  19.4 3.7 %collective-permute-start = (bf16[20,1,4,320]{3,2,1,0:T(4,128)(2,1)}, bf16[20,1,4,320]{3,2,1,0:T(4,128)(2,1)}, u32[]{:S(2)}, u32[]{:S(2)}) collective-permute-start(bf16[20,1,4,320]{3,2,1,0:T(4,128)(2,1)} %get-tuple-element.21), channel_id=1, source_target_pairs={{0,8},{8,16},{16,24},{1,9},{9,17},{17,25},{2,10},{10,18},{18,26},{... | collective-permute-start | bytes 153608 | tf_op jit(solution)/shard_map/ppermute | solution.py:19
  29.1 34.6 %all-gather = f32[160,4,32]{2,1,0:T(4,128)S(1)} all-gather(f32[10,4,32]{2,1,0:T(4,128)S(1)} %maximum_reduce_fusion), channel_id=2, replica_groups=mesh['gy'=4,'gx'=4,'probe'=2] {'gy','gx'}, dimensions={0}, use_global_device_ids=true | all-gather | bytes 87040 | tf_op jit(solution)/shard_map/all_gather | solution.py:10
  64.9 1.5 reshape.118
  71.6 4.6 %collective-permute-start.2 = (bf16[20,6,1,320]{3,2,1,0:T(2,128)(2,1)S(1)}, bf16[20,6,1,320]{3,2,1,0:T(2,128)(2,1)S(1)}, u32[]{:S(2)}, u32[]{:S(2)}) collective-permute-start(bf16[20,6,1,320]{3,2,1,0:T(2,128)(2,1)S(1)} %get-tuple-element.19), channel_id=1, source_target_pairs={{0,2},{2,4},{4,6},{1,3},{3,5},{5,7},{8,10},{10,12},{12,14},{9,11},... | collective-permute-start | bytes 230408 | tf_op jit(solution)/shard_map/ppermute | solution.py:19
  76.3 1.5 collective-permute-done.3
  77.8 1.5 collective-permute-done.2
  79.2 1.7 select_bitcast_fusion
  105.6 1.9 convolution_add_fusion.8
  107.5 1.6 reshape.128
  109.1 1.5 fusion.2
  111.8 1.7 fusion.64
  115.7 1.7 reshape.131
  117.4 1.7 reshape.132
  119.1 1.7 reshape.133
  120.8 1.7 reshape.134
  122.5 1.7 reshape.135
  124.2 1.7 reshape.136
  125.9 1.7 reshape.137
  127.6 1.7 reshape.138
  129.3 1.6 convolution_add_fusion.7
  130.9 1.5 convolution_add_fusion.6
  138.1 42.1 %psum.15 = f32[4]{0:T(128)S(1)} all-reduce(f32[4]{0:T(128)S(1)} %fusion.1), channel_id=1, replica_groups=mesh['gy'=4,'gx'=4,'probe'=2] {'gy','gx','probe'}, use_global_device_ids=true, to_apply=%region_8.9 | all-reduce | flops 4 | bytes 32 | tf_op jit(solution)/shard_map/psum | solution.py:99
  180.7 1.7 add_convert_fusion
  (98 shorter events, 50.8 us)
Async XLA Ops:
  7.2 59.3 %copy-start = (f32[1000,640]{1,0:T(8,128)S(1)}, f32[1000,640]{1,0:T(8,128)}, u32[]{:S(2)}) copy-start(f32[1000,640]{1,0:T(8,128)} %param.11) | copy-start | bytes 7680004
  7.2 59.3 %copy-start.15 = (s32[4]{0:T(128)S(1)}, s32[4]{0:T(128)}, u32[]{:S(2)}) copy-start(s32[4]{0:T(128)} %param.10) | copy-start | bytes 52
  7.2 173.5 %all-reduce.2.cloned.1.call-start = ((), (), s32[]{:S(2)}) async-start(), calls=%async_computation | async-start | bytes 327680 | tf_op jit(solution)/shard_map/psum | solution.py:94
  18.1 50.9 %collective-permute-start.1 = (bf16[20,1,4,320]{3,2,1,0:T(4,128)(2,1)}, bf16[20,1,4,320]{3,2,1,0:T(4,128)(2,1)S(1)}, u32[]{:S(2)}, u32[]{:S(2)}) collective-permute-start(bf16[20,1,4,320]{3,2,1,0:T(4,128)(2,1)} %get-tuple-element.22), channel_id=1, source_target_pairs={{8,0},{16,8},{24,16},{9,1},{17,9},{25,17},{10,2},{18,10},{26,18},{... | collective-permute-start | bytes 153608 | tf_op jit(solution)/shard_map/ppermute | solution.py:22
  19.4 49.6 %collective-permute-start = (bf16[20,1,4,320]{3,2,1,0:T(4,128)(2,1)}, bf16[20,1,4,320]{3,2,1,0:T(4,128)(2,1)}, u32[]{:S(2)}, u32[]{:S(2)}) collective-permute-start(bf16[20,1,4,320]{3,2,1,0:T(4,128)(2,1)} %get-tuple-element.21), channel_id=1, source_target_pairs={{0,8},{8,16},{16,24},{1,9},{9,17},{17,25},{2,10},{10,18},{18,26},{... | collective-permute-start | bytes 153608 | tf_op jit(solution)/shard_map/ppermute | solution.py:19
  23.9 44.3 %copy-start.14 = (f32[640]{0:T(1024)S(1)}, f32[640]{0:T(1024)}, u32[]{:S(2)}) copy-start(f32[640]{0:T(1024)} %param.12) | copy-start | bytes 7684
  70.3 7.4 %collective-permute-start.3 = (bf16[20,6,1,320]{3,2,1,0:T(2,128)(2,1)S(1)}, bf16[20,6,1,320]{3,2,1,0:T(2,128)(2,1)S(1)}, u32[]{:S(2)}, u32[]{:S(2)}) collective-permute-start(bf16[20,6,1,320]{3,2,1,0:T(2,128)(2,1)S(1)} %get-tuple-element.20), channel_id=1, source_target_pairs={{2,0},{4,2},{6,4},{3,1},{5,3},{7,5},{10,8},{12,10},{14,12},{11,9},... | collective-permute-start | bytes 230408 | tf_op jit(solution)/shard_map/ppermute | solution.py:22
  71.6 7.6 %collective-permute-start.2 = (bf16[20,6,1,320]{3,2,1,0:T(2,128)(2,1)S(1)}, bf16[20,6,1,320]{3,2,1,0:T(2,128)(2,1)S(1)}, u32[]{:S(2)}, u32[]{:S(2)}) collective-permute-start(bf16[20,6,1,320]{3,2,1,0:T(2,128)(2,1)S(1)} %get-tuple-element.19), channel_id=1, source_target_pairs={{0,2},{2,4},{4,6},{1,3},{3,5},{5,7},{8,10},{10,12},{12,14},{9,11},... | collective-permute-start | bytes 230408 | tf_op jit(solution)/shard_map/ppermute | solution.py:19
  77.8 3.2 %copy-start.7 = (bf16[20,6,1,320]{3,2,1,0:T(2,128)(2,1)}, bf16[20,6,1,320]{3,2,1,0:T(2,128)(2,1)S(1)}, u32[]{:S(2)}) copy-start(bf16[20,6,1,320]{3,2,1,0:T(2,128)(2,1)S(1)} %collective-permute-done.3) | copy-start | bytes 230404
  79.2 2.6 %copy-start.8 = (bf16[20,6,1,320]{3,2,1,0:T(2,128)(2,1)}, bf16[20,6,1,320]{3,2,1,0:T(2,128)(2,1)S(1)}, u32[]{:S(2)}) copy-start(bf16[20,6,1,320]{3,2,1,0:T(2,128)(2,1)S(1)} %collective-permute-done.2) | copy-start | bytes 230404
  95.7 6.3 %copy-start.12 = (bf16[64,320]{1,0:T(8,128)(2,1)S(1)}, bf16[64,320]{1,0:T(8,128)(2,1)}, u32[]{:S(2)}) copy-start(bf16[64,320]{1,0:T(8,128)(2,1)} %reshape.124) | copy-start | bytes 122884
  95.7 7.5 %copy-start.11 = (bf16[64,320]{1,0:T(8,128)(2,1)S(1)}, bf16[64,320]{1,0:T(8,128)(2,1)}, u32[]{:S(2)}) copy-start(bf16[64,320]{1,0:T(8,128)(2,1)} %reshape.125) | copy-start | bytes 122884
  95.7 8.7 %copy-start.9 = (bf16[64,320]{1,0:T(8,128)(2,1)S(1)}, bf16[64,320]{1,0:T(8,128)(2,1)}, u32[]{:S(2)}) copy-start(bf16[64,320]{1,0:T(8,128)(2,1)} %reshape.126) | copy-start | bytes 122884
  95.7 9.9 %copy-start.10 = (bf16[64,320]{1,0:T(8,128)(2,1)S(1)}, bf16[64,320]{1,0:T(8,128)(2,1)}, u32[]{:S(2)}) copy-start(bf16[64,320]{1,0:T(8,128)(2,1)} %reshape.127) | copy-start | bytes 122884
  129.3 3.1 %copy-start.1 = (bf16[9,320,640]{2,1,0:T(8,128)(2,1)S(1)}, bf16[9,320,640]{2,1,0:T(8,128)(2,1)}, u32[]{:S(2)}) copy-start(bf16[9,320,640]{2,1,0:T(8,128)(2,1)} %param.14) | copy-start | bytes 11059204
  129.3 4.5 %copy-start.6 = (bf16[256,320]{1,0:T(8,128)(2,1)S(1)}, bf16[256,320]{1,0:T(8,128)(2,1)}, u32[]{:S(2)}) copy-start(bf16[256,320]{1,0:T(8,128)(2,1)} %reshape.134) | copy-start | bytes 491524
  129.3 4.8 %copy-start.5 = (bf16[256,320]{1,0:T(8,128)(2,1)S(1)}, bf16[256,320]{1,0:T(8,128)(2,1)}, u32[]{:S(2)}) copy-start(bf16[256,320]{1,0:T(8,128)(2,1)} %reshape.135) | copy-start | bytes 491524
  130.9 3.6 %copy-start.4 = (bf16[256,320]{1,0:T(8,128)(2,1)S(1)}, bf16[256,320]{1,0:T(8,128)(2,1)}, u32[]{:S(2)}) copy-start(bf16[256,320]{1,0:T(8,128)(2,1)} %reshape.136) | copy-start | bytes 491524
  132.4 2.5 %copy-start.2 = (bf16[256,320]{1,0:T(8,128)(2,1)S(1)}, bf16[256,320]{1,0:T(8,128)(2,1)}, u32[]{:S(2)}) copy-start(bf16[256,320]{1,0:T(8,128)(2,1)} %reshape.137) | copy-start | bytes 491524
  133.7 1.5 copy-start.3
  134.5 46.2 %copy-start.13 = (f32[640]{0:T(1024)S(1)}, f32[640]{0:T(1024)}, u32[]{:S(2)}) copy-start(f32[640]{0:T(1024)} %param.15) | copy-start | bytes 7684
Sparse Core Ops, SparseCore 0:
  138.2 23.2 all-reduce.1
